TPU v7x, 32 devices: a whole 2x2x4 slice. The times are simulated.
32 devices in a mesh: blk: 16 (over z, x, core), rep: 2 (over y).
Axes of the slice: x: 2, y: 2, z: 4, core: 2. Of those that a mesh axis runs over, the one named last changes fastest.
Arguments:
- features: bfloat16 [4096, 128], P(('blk', 'rep')), may hold values from -6 to 6
- tile_mask: int32 [32, 32], P('blk'), may hold values 0 or 1
- multiplicity: int32 [32, 32], P('blk'), may hold values from 1 to 4
- w_query: bfloat16 [128, 128], replicated, may hold values from -0.5 to 0.5
- w_value: bfloat16 [128, 128], replicated, may hold values from -0.5 to 0.5
Outputs:
- updated: bfloat16 [4096, 128], P(('blk', 'rep'))
All inputs are finite; a program needn't handle non-finite values. No bound on the sum of `tile_mask` on one device may be relied on, other than what follows from the above.
Results may differ from a plain program's by a relative error of at most 0.0057.
Values may be sent and summed in bfloat16 or wider, within the bound.
A program may use at most 64 MiB of HBM per device.

v0:
```python
import math
import jax
import jax.numpy as jnp
from jax import lax
from jax.sharding import PartitionSpec as P

TILE = 128


def body(features, tile_mask, multiplicity, w_query, w_value):
    src_rows = features.shape[0]
    cycle_count = lax.axis_size("blk")
    rep_count = lax.axis_size("rep")
    rep_index = lax.axis_index("rep")
    own_query = jnp.dot(features, w_query, preferred_element_type=jnp.float32).astype(jnp.bfloat16)
    queries = lax.all_gather(own_query, "rep", axis=0, tiled=True)
    tgt_rows = queries.shape[0]
    tgt_tiles = tgt_rows // TILE
    src_tiles = src_rows // TILE
    factor = (tile_mask * multiplicity).astype(jnp.float32)
    factor = factor.reshape(tgt_tiles, cycle_count, rep_count, src_tiles)
    factor = lax.dynamic_index_in_dim(factor, rep_index, 2, keepdims=False)
    root_scale = 1.0 / features.shape[1] ** 0.5

    def absorb_tiles(partial_value, source, tile_factor):
        count_rows = source.shape[0]
        scores = (
            lax.dot_general(
                queries, source, (((1,), (1,)), ((), ())), preferred_element_type=jnp.float32
            )
            * root_scale
        )
        scores = jnp.where(scores > 0, scores, 0.2 * scores)
        weights = (
            scores.reshape(tgt_tiles, TILE, count_rows // TILE, TILE)
            * tile_factor[:, None, :, None]
        )
        weights = weights.reshape(tgt_rows, count_rows).astype(jnp.bfloat16)
        return partial_value + jnp.dot(weights, source, preferred_element_type=jnp.float32)

    start = jnp.zeros((tgt_rows, features.shape[1]), jnp.float32)
    flat_factor = factor.reshape(tgt_tiles, cycle_count * src_tiles)
    piece = lax.all_gather(features, "blk", axis=0, tiled=True)
    piece_rows = piece.shape[0]
    step_rows = math.gcd(piece_rows, max(src_rows, 1024))
    step_count = piece_rows // step_rows
    piece_blocks = piece.reshape(step_count, step_rows, piece.shape[1])

    def one_part(carry, index_pair):
        part_rows, part_index = index_pair
        first_tile = part_index * step_rows // TILE
        tile_factor = lax.dynamic_slice_in_dim(flat_factor, first_tile, step_rows // TILE, 1)
        return (absorb_tiles(carry, part_rows, tile_factor), None)

    result, unused = lax.scan(
        one_part, start, (piece_blocks, jnp.arange(step_count, dtype=jnp.int32))
    )
    partial_value = result
    summed = lax.psum_scatter(partial_value, "rep", scatter_dimension=0, tiled=True)
    total_verts = src_rows * cycle_count * rep_count
    aggregate = (summed * (2.0 * total_verts) ** (-0.5)).astype(jnp.bfloat16)
    mixed = jnp.dot(aggregate, w_value, preferred_element_type=jnp.float32)
    return (features.astype(jnp.float32) + mixed).astype(jnp.bfloat16)


def solution(mesh):
    in_specs = (P(("blk", "rep"), None), P("blk", None), P("blk", None), P(), P())
    out_specs = P(("blk", "rep"), None)
    return jax.shard_map(body, mesh=mesh, in_specs=in_specs, out_specs=out_specs, check_vma=False)
```

profile of v0, /device:TPU:0, one launch (start us, length us, event | category | flops | bytes accessed | tf_op | source)
XLA Modules:
  0.0 58.8 jit_solution(14389451639451653202)
XLA Ops:
  6.5 0.0 copy-start
  6.5 0.0 reduce-scatter.2.cloned.1.call-start
  6.5 0.0 copy-start.5
  6.5 0.0 copy-start.4
  6.6 0.7 %copy-done.5 = s32[2,32]{1,0:T(2,128)S(1)} copy-done((s32[2,32]{1,0:T(2,128)S(1)}, s32[2,32]{1,0:T(2,128)}, u32[]{:S(2)}) %copy-start.5) | copy-done | bytes 280
  7.2 0.0 copy-done.4
  7.3 0.1 reshape.20
  7.3 0.0 copy-start.1
  7.3 0.1 constant_dynamic-slice_fusion.1
  7.4 0.2 copy.8
  7.6 0.5 copy-done.1
  8.1 24.6 %all_gather.6 = bf16[2048,128]{1,0:T(8,128)(2,1)S(1)} all-gather(bf16[128,128]{1,0:T(8,128)(2,1)S(1)} %copy-done.1), channel_id=1, replica_groups=mesh['blk'=16,'rep'=2] {'blk'}, dimensions={0}, use_global_device_ids=true | all-gather | bytes 557056 | tf_op jit(solution)/shard_map/all_gather | solution.py:43
  32.7 0.0 copy-done
  32.7 0.1 convolution_convert_fusion
  32.8 4.6 %all_gather.7 = bf16[256,128]{1,0:T(8,128)(2,1)S(1)} all-gather(bf16[128,128]{1,0:T(8,128)(2,1)S(1)} %convolution_convert_fusion), channel_id=1, replica_groups=mesh['blk'=16,'rep'=2] {'rep'}, dimensions={0}, use_global_device_ids=true | all-gather | bytes 98304 | tf_op jit(solution)/shard_map/all_gather | solution.py:16
  37.4 4.4 %while.13 = (s32[]{:T(128)}, f32[256,128]{1,0:T(8,128)S(1)}, bf16[2,1024,128]{2,1,0:T(8,128)(2,1)S(1)}, bf16[256,128]{1,0:T(8,128)(2,1)S(1)}, s32[2]{0:T(128)S(1...) while((s32[]{:T(128)}, f32[256,128]{1,0:T(8,128)S(1)}, ...), condition=%wide.region_1.2_spmd.clone, body=%wide.region_0.1_spmd.clone.sunk | while | flops 135856144 | bytes 2950683 | solution.py:55
  37.4 0.6 dynamic_slice.44
  38.6 0.3 mul.98
  38.9 0.7 %convolution_add_fusion.3 = f32[256,128]{1,0:T(8,128)S(1)} fusion(f32[128,8,2,128]{3,2,1,0:T(2,128)S(1)} %bitcast.43, bf16[256,128]{1,0:T(8,128)(2,1)S(1)} %get-tuple-element.196, bf16[2,1024,128]{2,1,0:T(8,128)(2,1)S(1)} %get-tuple-element.195, s32[]{:T(128)} %get-tuple-element.180, f32[256,128]{1,0:T(8,128)S(1)} %get-tuple-element.181, pred[]{:T(512)S(6)} %compare.9), kind=kOutput, calls=%fused_computation.1.clone.1 | convolution fusion | flops 135856128 | bytes 1901569 | tf_op jit(solution)/shard_map/while/body/eval_jaxpr/dot_general | solution.py:39
  39.6 0.6 dynamic_slice.44
  40.8 0.3 mul.98
  41.2 0.7 %convolution_add_fusion.3 = f32[256,128]{1,0:T(8,128)S(1)} fusion(f32[128,8,2,128]{3,2,1,0:T(2,128)S(1)} %bitcast.43, bf16[256,128]{1,0:T(8,128)(2,1)S(1)} %get-tuple-element.196, bf16[2,1024,128]{2,1,0:T(8,128)(2,1)S(1)} %get-tuple-element.195, s32[]{:T(128)} %get-tuple-element.180, f32[256,128]{1,0:T(8,128)S(1)} %get-tuple-element.181, pred[]{:T(512)S(6)} %compare.9), kind=kOutput, calls=%fused_computation.1.clone.1 | convolution fusion | flops 135856128 | bytes 1901569 | tf_op jit(solution)/shard_map/while/body/eval_jaxpr/dot_general | solution.py:39
  41.8 0.0 copy-start.2
  41.9 0.0 copy-start.3
  41.9 0.6 %copy-done.2 = f32[256,128]{1,0:T(8,128)} copy-done((f32[256,128]{1,0:T(8,128)}, f32[256,128]{1,0:T(8,128)S(1)}, u32[]{:S(2)}) %copy-start.2) | copy-done | bytes 131096
  42.5 0.0 reduce-scatter.2.cloned.1.call-update
  42.5 7.8 %reduce-scatter.2.cloned.1.call-done = f32[128,128]{1,0:T(8,128)} async-done(((f32[256,128]{1,0:T(8,128)}), f32[128,128]{1,0:T(8,128)}) %reduce-scatter.2.cloned.1.call-update) | async-done | bytes 65552 | tf_op jit(solution)/shard_map/reduce_scatter | solution.py:59
  50.3 0.0 copy-done.3
  50.3 1.6 %fusion.14 = bf16[128,128]{1,0:T(8,128)(2,1)} fusion(bf16[128,128]{1,0:T(8,128)(2,1)S(1)} %copy-done.3, bf16[128,128]{1,0:T(8,128)(2,1)S(1)} %copy-done.1, f32[128,128]{1,0:T(8,128)} %reduce-scatter.2.cloned.1.call-done), kind=kOutput, calls=%fused_computation.15 | convolution fusion | flops 4276224 | bytes 163840 | tf_op jit(solution)/shard_map/dot_general | solution.py:62
  (5 shorter events, 0.0 us)
Async XLA Ops:
  6.5 26.2 %copy-start = (bf16[128,128]{1,0:T(8,128)(2,1)S(1)}, bf16[128,128]{1,0:T(8,128)(2,1)}, u32[]{:S(2)}) copy-start(bf16[128,128]{1,0:T(8,128)(2,1)} %param.10) | copy-start | bytes 98308
  6.5 43.8 %reduce-scatter.2.cloned.1.call-start = ((), (), s32[]{:S(2)}) async-start(), calls=%async_computation.1 | async-start | bytes 196608 | tf_op jit(solution)/shard_map/reduce_scatter | solution.py:59
  6.5 0.7 %copy-start.5 = (s32[2,32]{1,0:T(2,128)S(1)}, s32[2,32]{1,0:T(2,128)}, u32[]{:S(2)}) copy-start(s32[2,32]{1,0:T(2,128)} %param.9) | copy-start | bytes 772
  6.5 0.7 %copy-start.4 = (s32[2,32]{1,0:T(2,128)S(1)}, s32[2,32]{1,0:T(2,128)}, u32[]{:S(2)}) copy-start(s32[2,32]{1,0:T(2,128)} %param.8) | copy-start | bytes 772
  7.3 0.8 %copy-start.1 = (bf16[128,128]{1,0:T(8,128)(2,1)S(1)}, bf16[128,128]{1,0:T(8,128)(2,1)}, u32[]{:S(2)}) copy-start(bf16[128,128]{1,0:T(8,128)(2,1)} %param.7) | copy-start | bytes 98308
  41.8 0.7 %copy-start.2 = (f32[256,128]{1,0:T(8,128)}, f32[256,128]{1,0:T(8,128)S(1)}, u32[]{:S(2)}) copy-start(f32[256,128]{1,0:T(8,128)S(1)} %get-tuple-element.84) | copy-start | bytes 393220
  41.9 8.5 %copy-start.3 = (bf16[128,128]{1,0:T(8,128)(2,1)S(1)}, bf16[128,128]{1,0:T(8,128)(2,1)}, u32[]{:S(2)}) copy-start(bf16[128,128]{1,0:T(8,128)(2,1)} %param.11) | copy-start | bytes 98308
Sparse Core Ops, SparseCore 0:
  42.6 7.6 reduce-scatter.1
where the time goes:
time: 59.1 us; the launch traced here: 58.8 us
  blocking collectives  29.2 us (49%)
  between operations  13.4 us (23%)
  waiting for transfers between devices  7.82 us (13%)
  local copies, waits for them, and re-layouts  4.05 us (7%)
  matrix products  3.05 us (5%)
  loops' own time  1.24 us (2%)
    all_gather x1, blocking collectives, body(): piece = lax.all_gather(features, 'blk', axis=0, tiled=True)  24.6 us
    reduce_scatter x1, waiting for transfers between devices, body(): lax.psum_scatter(partial_value, 'rep', scatter_dimension=0, tiled=True)  7.8 us
    all_gather x1, blocking collectives, body(): queries = lax.all_gather(own_query, 'rep', axis=0, tiled=True)  4.58 us
    unnamed x13, local copies, waits for them, and re-layouts  2.02 us
    dot_general x1, matrix products, body(): mixed = jnp.dot(aggregate, w_value, preferred_element_type=jnp.float32)  1.59 us
    dot_general x2, matrix products, absorb_tiles(): jnp.dot(weights, source, preferred_element_type=jnp.float32)  1.33 us
    another operation x1, loops' own time, body(): lax.scan(one_part, start, (piece_blocks, jnp.arange(step_count, dtype=jnp...  1.24 us
  transfers between devices with their start and end apart: 1, of which 1 were waited for; matrix products, arithmetic and copies ran while one was open for 0% of the time, Pallas kernels for 0%

commit v1 on v0

--- a/solution.py
+++ b/solution.py
@@ -5,6 +5,22 @@
 from jax.sharding import PartitionSpec as P
 
 TILE = 128
+
+
+def _move_array(x_part):
+    width = lax.axis_size("blk")
+    formed = sorted(((u, (u + 1) % width) for u in range(width)))
+    heard = x_part
+    sides = [heard]
+    idx = 1
+    while idx < width:
+        heard = lax.ppermute(heard, axis_name="blk", perm=formed)
+        sides.insert(0, heard)
+        idx += 1
+    local_next = jnp.concatenate(sides, axis=0)
+    y1 = lax.axis_index("blk") + 1
+    d_next = jnp.roll(local_next, y1 * x_part.shape[0], axis=0)
+    return d_next
 
 
 def body(features, tile_mask, multiplicity, w_query, w_value):
@@ -40,7 +56,7 @@
 
     start = jnp.zeros((tgt_rows, features.shape[1]), jnp.float32)
     flat_factor = factor.reshape(tgt_tiles, cycle_count * src_tiles)
-    piece = lax.all_gather(features, "blk", axis=0, tiled=True)
+    piece = _move_array(features)
     piece_rows = piece.shape[0]
     step_rows = math.gcd(piece_rows, max(src_rows, 1024))
     step_count = piece_rows // step_rows

time: 59.1 us -> 124 us (2.10)
  waiting for transfers between devices: 7.82 us -> 95.3 us
  blocking collectives: 29.2 us -> 4.57 us
    ppermute x0 -> x15, waiting for transfers between devices: none -> 85.4 us  [_move_array(): heard = lax.ppermute(heard, axis_name='blk', perm=formed)]
    all_gather x1 -> x0, blocking collectives: 24.6 us -> none  [body(): piece = lax.all_gather(features, 'blk', axis=0, tiled=True)]
    reduce_scatter x1, waiting for transfers between devices: 7.8 us -> 9.85 us  [body(): lax.psum_scatter(partial_value, 'rep', scatter_dimension=0, tiled=True)]
  transfers between devices with their start and end apart: 1 -> 16, of which waited for: 1 -> 16; matrix products, arithmetic and copies ran while one was open for 0% -> 1% of each run, Pallas kernels for 0% -> 0%
where the time goes in v1:
time: 124 us; the launch traced here: 123 us
  waiting for transfers between devices  95.3 us (77%)
  between operations  13.6 us (11%)
  blocking collectives  4.57 us (4%)
  local copies, waits for them, and re-layouts  4.04 us (3%)
  matrix products  3.81 us (3%)
  loops' own time  1.4 us (1%)
    ppermute x15, waiting for transfers between devices, _move_array(): heard = lax.ppermute(heard, axis_name='blk', perm=formed)  85.4 us
    reduce_scatter x1, waiting for transfers between devices, body(): lax.psum_scatter(partial_value, 'rep', scatter_dimension=0, tiled=True)  9.85 us
    all_gather x1, blocking collectives, body(): queries = lax.all_gather(own_query, 'rep', axis=0, tiled=True)  4.57 us
  transfers between devices with their start and end apart: 16, of which 16 were waited for; matrix products, arithmetic and copies ran while one was open for 1% of the time, Pallas kernels for 0%

profile of v1, /device:TPU:0, one launch (start us, length us, event | category | flops | bytes accessed | tf_op | source)
XLA Modules:
  0.0 123.3 jit_solution(4713297066377542574)
XLA Ops:
  6.5 0.5 collective-permute-start
  7.1 6.8 %collective-permute-done = bf16[128,128]{1,0:T(8,128)(2,1)S(1)} collective-permute-done((bf16[128,128]{1,0:T(8,128)(2,1)}, bf16[128,128]{1,0:T(8,128)(2,1)S(1)}, u32[]{:S(2)}, u32[]{:S(2)}) %collective-permute-start) | collective-permute-done | bytes 32800 | tf_op jit(solution)/shard_map/ppermute | solution.py:17
  13.9 6.0 %collective-permute-done.1 = bf16[128,128]{1,0:T(8,128)(2,1)S(1)} collective-permute-done((bf16[128,128]{1,0:T(8,128)(2,1)S(1)}, bf16[128,128]{1,0:T(8,128)(2,1)S(1)}, u32[]{:S(2)}, u32[]{:S(2)}) %collective-permute-start.1) | collective-permute-done | bytes 32800 | tf_op jit(solution)/shard_map/ppermute | solution.py:17
  19.9 6.0 %collective-permute-done.2 = bf16[128,128]{1,0:T(8,128)(2,1)S(1)} collective-permute-done((bf16[128,128]{1,0:T(8,128)(2,1)S(1)}, bf16[128,128]{1,0:T(8,128)(2,1)S(1)}, u32[]{:S(2)}, u32[]{:S(2)}) %collective-permute-start.2) | collective-permute-done | bytes 32800 | tf_op jit(solution)/shard_map/ppermute | solution.py:17
  25.9 6.0 %collective-permute-done.3 = bf16[128,128]{1,0:T(8,128)(2,1)S(1)} collective-permute-done((bf16[128,128]{1,0:T(8,128)(2,1)S(1)}, bf16[128,128]{1,0:T(8,128)(2,1)S(1)}, u32[]{:S(2)}, u32[]{:S(2)}) %collective-permute-start.3) | collective-permute-done | bytes 32800 | tf_op jit(solution)/shard_map/ppermute | solution.py:17
  32.0 6.0 %collective-permute-done.4 = bf16[128,128]{1,0:T(8,128)(2,1)S(1)} collective-permute-done((bf16[128,128]{1,0:T(8,128)(2,1)S(1)}, bf16[128,128]{1,0:T(8,128)(2,1)S(1)}, u32[]{:S(2)}, u32[]{:S(2)}) %collective-permute-start.4) | collective-permute-done | bytes 32800 | tf_op jit(solution)/shard_map/ppermute | solution.py:17
  38.0 6.0 %collective-permute-done.5 = bf16[128,128]{1,0:T(8,128)(2,1)S(1)} collective-permute-done((bf16[128,128]{1,0:T(8,128)(2,1)S(1)}, bf16[128,128]{1,0:T(8,128)(2,1)S(1)}, u32[]{:S(2)}, u32[]{:S(2)}) %collective-permute-start.5) | collective-permute-done | bytes 32800 | tf_op jit(solution)/shard_map/ppermute | solution.py:17
  44.0 6.0 %collective-permute-done.6 = bf16[128,128]{1,0:T(8,128)(2,1)S(1)} collective-permute-done((bf16[128,128]{1,0:T(8,128)(2,1)S(1)}, bf16[128,128]{1,0:T(8,128)(2,1)S(1)}, u32[]{:S(2)}, u32[]{:S(2)}) %collective-permute-start.6) | collective-permute-done | bytes 32800 | tf_op jit(solution)/shard_map/ppermute | solution.py:17
  50.1 6.0 %collective-permute-done.7 = bf16[128,128]{1,0:T(8,128)(2,1)S(1)} collective-permute-done((bf16[128,128]{1,0:T(8,128)(2,1)S(1)}, bf16[128,128]{1,0:T(8,128)(2,1)S(1)}, u32[]{:S(2)}, u32[]{:S(2)}) %collective-permute-start.7) | collective-permute-done | bytes 32800 | tf_op jit(solution)/shard_map/ppermute | solution.py:17
  56.1 6.0 %collective-permute-done.8 = bf16[128,128]{1,0:T(8,128)(2,1)S(1)} collective-permute-done((bf16[128,128]{1,0:T(8,128)(2,1)S(1)}, bf16[128,128]{1,0:T(8,128)(2,1)S(1)}, u32[]{:S(2)}, u32[]{:S(2)}) %collective-permute-start.8) | collective-permute-done | bytes 32800 | tf_op jit(solution)/shard_map/ppermute | solution.py:17
  62.2 6.0 %collective-permute-done.9 = bf16[128,128]{1,0:T(8,128)(2,1)S(1)} collective-permute-done((bf16[128,128]{1,0:T(8,128)(2,1)S(1)}, bf16[128,128]{1,0:T(8,128)(2,1)S(1)}, u32[]{:S(2)}, u32[]{:S(2)}) %collective-permute-start.9) | collective-permute-done | bytes 32800 | tf_op jit(solution)/shard_map/ppermute | solution.py:17
  68.2 6.0 %collective-permute-done.10 = bf16[128,128]{1,0:T(8,128)(2,1)S(1)} collective-permute-done((bf16[128,128]{1,0:T(8,128)(2,1)S(1)}, bf16[128,128]{1,0:T(8,128)(2,1)S(1)}, u32[]{:S(2)}, u32[]{:S(2)}) %collective-permute-start.10) | collective-permute-done | bytes 32800 | tf_op jit(solution)/shard_map/ppermute | solution.py:17
  74.2 6.0 %collective-permute-done.11 = bf16[128,128]{1,0:T(8,128)(2,1)S(1)} collective-permute-done((bf16[128,128]{1,0:T(8,128)(2,1)S(1)}, bf16[128,128]{1,0:T(8,128)(2,1)S(1)}, u32[]{:S(2)}, u32[]{:S(2)}) %collective-permute-start.11) | collective-permute-done | bytes 32800 | tf_op jit(solution)/shard_map/ppermute | solution.py:17
  80.3 0.9 convolution_convert_fusion
  81.2 5.1 %collective-permute-done.12 = bf16[128,128]{1,0:T(8,128)(2,1)S(1)} collective-permute-done((bf16[128,128]{1,0:T(8,128)(2,1)S(1)}, bf16[128,128]{1,0:T(8,128)(2,1)S(1)}, u32[]{:S(2)}, u32[]{:S(2)}) %collective-permute-start.12) | collective-permute-done | bytes 32800 | tf_op jit(solution)/shard_map/ppermute | solution.py:17
  86.3 0.1 reshape.20
  86.4 5.9 %collective-permute-done.13 = bf16[128,128]{1,0:T(8,128)(2,1)S(1)} collective-permute-done((bf16[128,128]{1,0:T(8,128)(2,1)S(1)}, bf16[128,128]{1,0:T(8,128)(2,1)S(1)}, u32[]{:S(2)}, u32[]{:S(2)}) %collective-permute-start.13) | collective-permute-done | bytes 32800 | tf_op jit(solution)/shard_map/ppermute | solution.py:17
  92.3 0.1 constant_dynamic-slice_fusion.1
  92.4 0.2 copy.8
  92.6 4.6 %all_gather.3 = bf16[256,128]{1,0:T(8,128)(2,1)S(1)} all-gather(bf16[128,128]{1,0:T(8,128)(2,1)S(1)} %convolution_convert_fusion), channel_id=1, replica_groups=mesh['blk'=16,'rep'=2] {'rep'}, dimensions={0}, use_global_device_ids=true | all-gather | bytes 98304 | tf_op jit(solution)/shard_map/all_gather | solution.py:32
  97.2 1.2 collective-permute-done.14
  98.6 0.7 copy-done.1
  99.6 4.7 %while.13 = (s32[]{:T(128)}, f32[256,128]{1,0:T(8,128)S(1)}, bf16[2,1024,128]{2,1,0:T(8,128)(2,1)S(1)}, bf16[256,128]{1,0:T(8,128)(2,1)S(1)}, s32[2]{0:T(128)S(1...) while((s32[]{:T(128)}, f32[256,128]{1,0:T(8,128)S(1)}, ...), condition=%wide.region_1.2_spmd.clone, body=%wide.region_0.1_spmd.clone.sunk | while | flops 135856144 | bytes 2950683 | solution.py:71
  99.7 0.6 dynamic_slice.50
  101.0 0.3 mul.102
  101.3 0.7 convolution_add_fusion.3
  102.0 0.6 dynamic_slice.50
  103.3 0.3 mul.102
  103.6 0.7 convolution_add_fusion.3
  104.3 0.6 copy-done.2
  105.0 9.8 %reduce-scatter.2.cloned.1.call-done = f32[128,128]{1,0:T(8,128)} async-done(((f32[256,128]{1,0:T(8,128)}), f32[128,128]{1,0:T(8,128)}) %reduce-scatter.2.cloned.1.call-update) | async-done | bytes 65552 | tf_op jit(solution)/shard_map/reduce_scatter | solution.py:75
  114.8 1.6 %fusion.14 = bf16[128,128]{1,0:T(8,128)(2,1)} fusion(bf16[128,128]{1,0:T(8,128)(2,1)S(1)} %copy-done.3, bf16[128,128]{1,0:T(8,128)(2,1)S(1)} %copy-done.1, f32[128,128]{1,0:T(8,128)} %reduce-scatter.2.cloned.1.call-done), kind=kOutput, calls=%fused_computation.15 | convolution fusion | flops 4276224 | bytes 163840 | tf_op jit(solution)/shard_map/dot_general | solution.py:78
  (64 shorter events, 0.5 us)
Async XLA Ops:
  6.5 73.7 %copy-start = (bf16[128,128]{1,0:T(8,128)(2,1)S(1)}, bf16[128,128]{1,0:T(8,128)(2,1)}, u32[]{:S(2)}) copy-start(bf16[128,128]{1,0:T(8,128)(2,1)} %param.10) | copy-start | bytes 98308
  6.5 79.8 %copy-start.4 = (s32[2,32]{1,0:T(2,128)S(1)}, s32[2,32]{1,0:T(2,128)}, u32[]{:S(2)}) copy-start(s32[2,32]{1,0:T(2,128)} %param.8) | copy-start | bytes 772
  6.5 79.8 %copy-start.5 = (s32[2,32]{1,0:T(2,128)S(1)}, s32[2,32]{1,0:T(2,128)}, u32[]{:S(2)}) copy-start(s32[2,32]{1,0:T(2,128)} %param.9) | copy-start | bytes 772
  6.5 108.3 %reduce-scatter.2.cloned.1.call-start = ((), (), s32[]{:S(2)}) async-start(), calls=%async_computation.1 | async-start | bytes 196608 | tf_op jit(solution)/shard_map/reduce_scatter | solution.py:75
  6.5 7.3 %collective-permute-start = (bf16[128,128]{1,0:T(8,128)(2,1)}, bf16[128,128]{1,0:T(8,128)(2,1)S(1)}, u32[]{:S(2)}, u32[]{:S(2)}) collective-permute-start(bf16[128,128]{1,0:T(8,128)(2,1)} %param.7), channel_id=1, source_target_pairs={{0,2},{2,4},{4,6},{6,8},{8,10},{10,12},{12,14},{14,16},{16,18},{18... | collective-permute-start | bytes 98312 | tf_op jit(solution)/shard_map/ppermute | solution.py:17
  13.9 6.0 %collective-permute-start.1 = (bf16[128,128]{1,0:T(8,128)(2,1)S(1)}, bf16[128,128]{1,0:T(8,128)(2,1)S(1)}, u32[]{:S(2)}, u32[]{:S(2)}) collective-permute-start(bf16[128,128]{1,0:T(8,128)(2,1)S(1)} %collective-permute-done), channel_id=1, source_target_pairs={{0,2},{2,4},{4,6},{6,8},{8,10},{10,12},{12,14},{14,16},{16,18},{18... | collective-permute-start | bytes 98312 | tf_op jit(solution)/shard_map/ppermute | solution.py:17
  19.9 6.0 %collective-permute-start.2 = (bf16[128,128]{1,0:T(8,128)(2,1)S(1)}, bf16[128,128]{1,0:T(8,128)(2,1)S(1)}, u32[]{:S(2)}, u32[]{:S(2)}) collective-permute-start(bf16[128,128]{1,0:T(8,128)(2,1)S(1)} %collective-permute-done.1), channel_id=1, source_target_pairs={{0,2},{2,4},{4,6},{6,8},{8,10},{10,12},{12,14},{14,16},{16,18},{18... | collective-permute-start | bytes 98312 | tf_op jit(solution)/shard_map/ppermute | solution.py:17
  25.9 6.0 %collective-permute-start.3 = (bf16[128,128]{1,0:T(8,128)(2,1)S(1)}, bf16[128,128]{1,0:T(8,128)(2,1)S(1)}, u32[]{:S(2)}, u32[]{:S(2)}) collective-permute-start(bf16[128,128]{1,0:T(8,128)(2,1)S(1)} %collective-permute-done.2), channel_id=1, source_target_pairs={{0,2},{2,4},{4,6},{6,8},{8,10},{10,12},{12,14},{14,16},{16,18},{18... | collective-permute-start | bytes 98312 | tf_op jit(solution)/shard_map/ppermute | solution.py:17
  32.0 6.0 %collective-permute-start.4 = (bf16[128,128]{1,0:T(8,128)(2,1)S(1)}, bf16[128,128]{1,0:T(8,128)(2,1)S(1)}, u32[]{:S(2)}, u32[]{:S(2)}) collective-permute-start(bf16[128,128]{1,0:T(8,128)(2,1)S(1)} %collective-permute-done.3), channel_id=1, source_target_pairs={{0,2},{2,4},{4,6},{6,8},{8,10},{10,12},{12,14},{14,16},{16,18},{18... | collective-permute-start | bytes 98312 | tf_op jit(solution)/shard_map/ppermute | solution.py:17
  38.0 6.0 %collective-permute-start.5 = (bf16[128,128]{1,0:T(8,128)(2,1)S(1)}, bf16[128,128]{1,0:T(8,128)(2,1)S(1)}, u32[]{:S(2)}, u32[]{:S(2)}) collective-permute-start(bf16[128,128]{1,0:T(8,128)(2,1)S(1)} %collective-permute-done.4), channel_id=1, source_target_pairs={{0,2},{2,4},{4,6},{6,8},{8,10},{10,12},{12,14},{14,16},{16,18},{18... | collective-permute-start | bytes 98312 | tf_op jit(solution)/shard_map/ppermute | solution.py:17
  44.0 6.0 %collective-permute-start.6 = (bf16[128,128]{1,0:T(8,128)(2,1)S(1)}, bf16[128,128]{1,0:T(8,128)(2,1)S(1)}, u32[]{:S(2)}, u32[]{:S(2)}) collective-permute-start(bf16[128,128]{1,0:T(8,128)(2,1)S(1)} %collective-permute-done.5), channel_id=1, source_target_pairs={{0,2},{2,4},{4,6},{6,8},{8,10},{10,12},{12,14},{14,16},{16,18},{18... | collective-permute-start | bytes 98312 | tf_op jit(solution)/shard_map/ppermute | solution.py:17
  50.1 6.0 %collective-permute-start.7 = (bf16[128,128]{1,0:T(8,128)(2,1)S(1)}, bf16[128,128]{1,0:T(8,128)(2,1)S(1)}, u32[]{:S(2)}, u32[]{:S(2)}) collective-permute-start(bf16[128,128]{1,0:T(8,128)(2,1)S(1)} %collective-permute-done.6), channel_id=1, source_target_pairs={{0,2},{2,4},{4,6},{6,8},{8,10},{10,12},{12,14},{14,16},{16,18},{18... | collective-permute-start | bytes 98312 | tf_op jit(solution)/shard_map/ppermute | solution.py:17
  56.1 6.0 %collective-permute-start.8 = (bf16[128,128]{1,0:T(8,128)(2,1)S(1)}, bf16[128,128]{1,0:T(8,128)(2,1)S(1)}, u32[]{:S(2)}, u32[]{:S(2)}) collective-permute-start(bf16[128,128]{1,0:T(8,128)(2,1)S(1)} %collective-permute-done.7), channel_id=1, source_target_pairs={{0,2},{2,4},{4,6},{6,8},{8,10},{10,12},{12,14},{14,16},{16,18},{18... | collective-permute-start | bytes 98312 | tf_op jit(solution)/shard_map/ppermute | solution.py:17
  62.2 6.0 %collective-permute-start.9 = (bf16[128,128]{1,0:T(8,128)(2,1)S(1)}, bf16[128,128]{1,0:T(8,128)(2,1)S(1)}, u32[]{:S(2)}, u32[]{:S(2)}) collective-permute-start(bf16[128,128]{1,0:T(8,128)(2,1)S(1)} %collective-permute-done.8), channel_id=1, source_target_pairs={{0,2},{2,4},{4,6},{6,8},{8,10},{10,12},{12,14},{14,16},{16,18},{18... | collective-permute-start | bytes 98312 | tf_op jit(solution)/shard_map/ppermute | solution.py:17
  68.2 6.0 %collective-permute-start.10 = (bf16[128,128]{1,0:T(8,128)(2,1)S(1)}, bf16[128,128]{1,0:T(8,128)(2,1)S(1)}, u32[]{:S(2)}, u32[]{:S(2)}) collective-permute-start(bf16[128,128]{1,0:T(8,128)(2,1)S(1)} %collective-permute-done.9), channel_id=1, source_target_pairs={{0,2},{2,4},{4,6},{6,8},{8,10},{10,12},{12,14},{14,16},{16,18},{18... | collective-permute-start | bytes 98312 | tf_op jit(solution)/shard_map/ppermute | solution.py:17
  74.2 6.0 %collective-permute-start.11 = (bf16[128,128]{1,0:T(8,128)(2,1)S(1)}, bf16[128,128]{1,0:T(8,128)(2,1)S(1)}, u32[]{:S(2)}, u32[]{:S(2)}) collective-permute-start(bf16[128,128]{1,0:T(8,128)(2,1)S(1)} %collective-permute-done.10), channel_id=1, source_target_pairs={{0,2},{2,4},{4,6},{6,8},{8,10},{10,12},{12,14},{14,16},{16,18},{18... | collective-permute-start | bytes 98312 | tf_op jit(solution)/shard_map/ppermute | solution.py:17
  80.3 6.0 %collective-permute-start.12 = (bf16[128,128]{1,0:T(8,128)(2,1)S(1)}, bf16[128,128]{1,0:T(8,128)(2,1)S(1)}, u32[]{:S(2)}, u32[]{:S(2)}) collective-permute-start(bf16[128,128]{1,0:T(8,128)(2,1)S(1)} %collective-permute-done.11), channel_id=1, source_target_pairs={{0,2},{2,4},{4,6},{6,8},{8,10},{10,12},{12,14},{14,16},{16,18},{18... | collective-permute-start | bytes 98312 | tf_op jit(solution)/shard_map/ppermute | solution.py:17
  86.3 6.0 %collective-permute-start.13 = (bf16[128,128]{1,0:T(8,128)(2,1)S(1)}, bf16[128,128]{1,0:T(8,128)(2,1)S(1)}, u32[]{:S(2)}, u32[]{:S(2)}) collective-permute-start(bf16[128,128]{1,0:T(8,128)(2,1)S(1)} %collective-permute-done.12), channel_id=1, source_target_pairs={{0,2},{2,4},{4,6},{6,8},{8,10},{10,12},{12,14},{14,16},{16,18},{18... | collective-permute-start | bytes 98312 | tf_op jit(solution)/shard_map/ppermute | solution.py:17
  92.3 6.0 %collective-permute-start.14 = (bf16[128,128]{1,0:T(8,128)(2,1)S(1)}, bf16[128,128]{1,0:T(8,128)(2,1)S(1)}, u32[]{:S(2)}, u32[]{:S(2)}) collective-permute-start(bf16[128,128]{1,0:T(8,128)(2,1)S(1)} %collective-permute-done.13), channel_id=1, source_target_pairs={{0,2},{2,4},{4,6},{6,8},{8,10},{10,12},{12,14},{14,16},{16,18},{18... | collective-permute-start | bytes 98312 | tf_op jit(solution)/shard_map/ppermute | solution.py:17
  98.6 0.8 copy-start.1
  104.3 0.7 copy-start.2
  104.3 10.5 %copy-start.3 = (bf16[128,128]{1,0:T(8,128)(2,1)S(1)}, bf16[128,128]{1,0:T(8,128)(2,1)}, u32[]{:S(2)}) copy-start(bf16[128,128]{1,0:T(8,128)(2,1)} %param.11) | copy-start | bytes 98308
Sparse Core Ops, SparseCore 0:
  105.1 9.6 reduce-scatter.1
